TPU v7x, 256 devices: a whole 4x4x8 slice. The times are simulated.
256 devices in a mesh: seq: 64 (over z, x, core), head: 4 (over y).
Axes of the slice: x: 4, y: 4, z: 8, core: 2. Of those that a mesh axis runs over, the one named last changes fastest.
Arguments:
- queries: bfloat16 [65536, 2048], P('seq', 'head'), may hold values from -14 to 14, as said below
- key_vectors: bfloat16 [65536, 2048], P('seq', 'head'), may hold values from -6 to 6
- value_vectors: bfloat16 [65536, 2048], P('seq', 'head'), may hold values from -20 to 20, as said below
- cotangent: bfloat16 [65536, 2048], P('seq', 'head'), may hold values from -6 to 6
- norm_gain: float32 [2048], P('head'), may hold values from 0.5 to 2
Outputs:
- mixed: bfloat16 [65536, 2048], P('seq', 'head')
- grad_queries: bfloat16 [65536, 2048], P('seq', 'head')
- grad_keys: bfloat16 [65536, 2048], P('seq', 'head')
- grad_values: bfloat16 [65536, 2048], P('seq', 'head')
Inputs may be any that keep to these rules, and one draw needn't show every extreme that they name: `queries`: real values. `value_vectors`: real values.
All inputs are finite; a program needn't handle non-finite values.
Results may differ from a plain program's by a relative error of at most 0.013.
Values may be sent and summed in bfloat16 or wider, within the bound.
No kernel may reach another device: no remote copies, remote signals or barrier semaphores. Data moves between devices by JAX's collectives and lax.ppermute only.
A program may use at most 128 MiB of HBM per device.

v0:
```python
import jax
import jax.numpy as jnp
from jax import lax
from jax.sharding import PartitionSpec as P

HEAD_DIM = 128
WIDTH = 2048
epsilon = 1e-06


def shards(queries, key_vectors, value_vectors, cotangent, norm_gain):
    tokens_here = queries.shape[0]
    columns = queries.shape[1]
    heads_here = columns // HEAD_DIM
    shaped_q = queries.reshape(tokens_here, heads_here, HEAD_DIM)
    shaped_k = key_vectors.reshape(tokens_here, heads_here, HEAD_DIM)
    shaped_v = value_vectors.reshape(tokens_here, heads_here, HEAD_DIM)
    block_state = jnp.einsum(
        "thd,the->hde", shaped_k, shaped_v, preferred_element_type=jnp.float32
    ).astype(jnp.bfloat16)
    position = lax.axis_index("seq")
    piece = lax.all_gather(block_state[None], "seq", axis=0, tiled=True)
    owners = jnp.arange(piece.shape[0], dtype=jnp.int32)
    select = (owners < position).astype(jnp.bfloat16)
    prefix = jnp.einsum("n,nhde->hde", select, piece, preferred_element_type=jnp.float32)
    prefix_bf = prefix.astype(jnp.bfloat16)
    causal = jnp.arange(tokens_here)[:, None] >= jnp.arange(tokens_here)[None, :]
    head_outputs = []
    head_weights = []
    for head_number in range(heads_here):
        lower = head_number * HEAD_DIM
        query_head = queries[:, lower : lower + HEAD_DIM]
        key_head = key_vectors[:, lower : lower + HEAD_DIM]
        value_head = value_vectors[:, lower : lower + HEAD_DIM]
        scores = jnp.dot(query_head, key_head.T, preferred_element_type=jnp.float32)
        weights = jnp.where(causal, scores, 0.0).astype(jnp.bfloat16)
        output = jnp.dot(weights, value_head, preferred_element_type=jnp.float32)
        output = output + jnp.dot(
            query_head, prefix_bf[head_number], preferred_element_type=jnp.float32
        )
        head_outputs.append(output)
        head_weights.append(weights)
    attn = jnp.concatenate(head_outputs, axis=1)
    upstream = cotangent.astype(jnp.float32) * norm_gain
    squares = jnp.sum(attn * attn, axis=1)
    local_dots = jnp.sum(upstream * attn, axis=1)
    square_total = lax.psum(squares, "head")
    inv = lax.rsqrt(square_total / WIDTH + epsilon)
    mixed = (attn * inv[:, None] * norm_gain).astype(jnp.bfloat16)
    dot_total = lax.psum(local_dots, "head")
    grad_attn = (
        inv[:, None] * (upstream - attn * (inv * inv * dot_total / WIDTH)[:, None])
    ).astype(jnp.bfloat16)
    grad_shaped = grad_attn.reshape(tokens_here, heads_here, HEAD_DIM)
    query_term = jnp.einsum(
        "thd,the->hde", shaped_q, grad_shaped, preferred_element_type=jnp.float32
    ).astype(jnp.bfloat16)
    piece = lax.all_gather(query_term[None], "seq", axis=0, tiled=True)
    owners = jnp.arange(piece.shape[0], dtype=jnp.int32)
    select = (owners > position).astype(jnp.bfloat16)
    suffix = jnp.einsum("n,nhde->hde", select, piece, preferred_element_type=jnp.float32)
    suffix_bf = suffix.astype(jnp.bfloat16)
    grads_q = []
    grads_k = []
    grads_v = []
    for head_number in range(heads_here):
        lower = head_number * HEAD_DIM
        query_head = queries[:, lower : lower + HEAD_DIM]
        key_head = key_vectors[:, lower : lower + HEAD_DIM]
        value_head = value_vectors[:, lower : lower + HEAD_DIM]
        grad_head = grad_attn[:, lower : lower + HEAD_DIM]
        dscores = jnp.dot(grad_head, value_head.T, preferred_element_type=jnp.float32)
        dweights = jnp.where(causal, dscores, 0.0).astype(jnp.bfloat16)
        grad_q = jnp.dot(dweights, key_head, preferred_element_type=jnp.float32)
        grad_q = grad_q + jnp.dot(
            grad_head, prefix_bf[head_number].T, preferred_element_type=jnp.float32
        )
        grad_k = jnp.dot(dweights.T, query_head, preferred_element_type=jnp.float32)
        grad_k = grad_k + jnp.dot(
            value_head, suffix_bf[head_number].T, preferred_element_type=jnp.float32
        )
        grad_v = jnp.dot(head_weights[head_number].T, grad_head, preferred_element_type=jnp.float32)
        grad_v = grad_v + jnp.dot(
            key_head, suffix_bf[head_number], preferred_element_type=jnp.float32
        )
        grads_q.append(grad_q.astype(jnp.bfloat16))
        grads_k.append(grad_k.astype(jnp.bfloat16))
        grads_v.append(grad_v.astype(jnp.bfloat16))
    return (
        mixed,
        jnp.concatenate(grads_q, axis=1),
        jnp.concatenate(grads_k, axis=1),
        jnp.concatenate(grads_v, axis=1),
    )


def solution(mesh):
    return jax.shard_map(
        shards,
        mesh=mesh,
        in_specs=(
            P("seq", "head"),
            P("seq", "head"),
            P("seq", "head"),
            P("seq", "head"),
            P("head"),
        ),
        out_specs=(P("seq", "head"), P("seq", "head"), P("seq", "head"), P("seq", "head")),
        check_vma=False,
    )
```

profile of v0, /device:TPU:1, one launch (start us, length us, event | category | flops | bytes accessed | tf_op | source)
XLA Modules:
  0.0 223.5 jit_solution(6410495051114955417)
XLA Ops:
  7.2 2.3 %copy.32 = bf16[1024,512]{0,1:T(8,128)(2,1)} copy(bf16[1024,512]{1,0:T(8,128)(2,1)} %param.6) | data formatting | bytes 2097152 | tf_op jit(solution)/shard_map/reshape | solution.py:16
  9.6 2.5 %convolution_convert_fusion.1 = bf16[4,128,128]{2,1,0:T(8,128)(2,1)} fusion(bf16[1024,4,128]{0,2,1:T(8,128)(2,1)} %bitcast.153, bf16[1024,512]{1,0:T(8,128)(2,1)S(1)} %copy-done.23), kind=kOutput, calls=%fused_computation.60 | convolution fusion | flops 134283264 | bytes 2228224 | tf_op jit(solution)/shard_map/thd,the->hde/dot_general | solution.py:18
  12.1 1.5 copy.19
  16.7 1.1 copy-done.24
  17.9 0.8 fusion.63
  18.7 1.6 fusion.75
  20.3 0.8 fusion.87
  21.2 0.8 fusion.51
  22.0 77.3 %all-gather.5.cloned.1.call-done = bf16[256,128,128]{2,1,0:T(8,128)(2,1)} async-done(((bf16[4,128,128]{2,1,0:T(8,128)(2,1)}), bf16[256,128,128]{2,1,0:T(8,128)(2,1)}) %all-gather.5.cloned.1.call-update) | async-done | bytes 8388624 | tf_op jit(solution)/shard_map/all_gather | solution.py:22
  99.3 8.1 %fusion.2 = f32[1,4,128,128]{3,0,2,1:T(1,128)S(1)} fusion(bf16[64,4,128,128]{3,2,1,0:T(8,128)(2,1)} %bitcast.150, s32[]{:T(128)S(6)} %axis_index.15), kind=kOutput, calls=%fused_computation.2 | convolution fusion | flops 8388672 | bytes 8650756 | tf_op jit(solution)/shard_map/n,nhde->hde/dot_general | solution.py:25
  110.0 8.5 %all-reduce = (f32[1024]{0:T(1024)S(1)}, f32[1024]{0:T(1024)S(1)}) all-reduce(f32[1024]{0:T(1024)S(1)} %get-tuple-element.13, f32[1024]{0:T(1024)S(1)} %get-tuple-element.12), channel_id=1, replica_groups=mesh['seq'=64,'head'=4] {'head'}, use_global_device_ids=true, to_apply=%region_1.2 | all-reduce | flops 2048 | bytes 16384 | tf_op jit(solution)/shard_map/psum | solution.py:47
  118.6 2.9 %multiply_convert_fusion = (bf16[1024,512]{0,1:T(8,128)(2,1)S(1)}, bf16[1024,512]{0,1:T(8,128)(2,1)}) fusion(bf16[1024,512]{0,1:T(8,128)(2,1)S(1)} %copy.19, f32[1024]{0:T(1024)S(1)} %get-tuple-element.18, f32[512]{0:T(512)S(1)} %copy-done.35, f32[1024]{0:T(1024)S(1)} %get-tuple-element.19, f32[1024,128]{0,1:T(8,128)} %copy-done.17, ...), kind=kLoop, calls=%fused_computation.14 | loop fusion | flops 6291456 | bytes 5253120 | tf_op jit(solution)/shard_map/convert_element_type | solution.py:53
  122.7 1.3 copy.22
  124.1 1.8 select_convert_fusion
  125.9 0.8 fusion.54
  127.9 0.8 fusion.66
  129.8 0.8 fusion.78
  131.7 0.8 fusion.90
  133.2 1.0 pad_maximum_fusion.1
  134.3 2.3 %copy.23 = bf16[1024,512]{1,0:T(8,128)(2,1)} copy(bf16[1024,512]{0,1:T(8,128)(2,1)} %pad_maximum_fusion.1) | data formatting | bytes 2097152
  136.6 3.0 %fusion.46 = f32[1024,128]{0,1:T(8,128)} fusion(bf16[1024,1024]{1,0:T(8,128)(2,1)} %copy-done.15, bf16[1024,512]{0,1:T(8,128)(2,1)S(1)} %get-tuple-element.16), kind=kOutput, calls=%fused_computation.82 | convolution fusion | flops 268435456 | bytes 2883584 | tf_op jit(solution)/shard_map/dot_general | solution.py:82
  139.6 1.3 fusion.42
  141.4 1.2 fusion.38
  143.2 1.2 fusion.34
  144.4 1.3 fusion.57
  146.7 1.1 copy-done.3
  147.8 1.3 fusion.81
  149.6 1.3 fusion.93
  150.8 51.7 %all-gather.7.cloned.1.call-done = bf16[256,128,128]{2,1,0:T(8,128)(2,1)} async-done(((bf16[4,128,128]{2,1,0:T(8,128)(2,1)}), bf16[256,128,128]{2,1,0:T(8,128)(2,1)}) %all-gather.7.cloned.1.call-update) | async-done | bytes 8388624 | tf_op jit(solution)/shard_map/all_gather | solution.py:58
  202.6 8.1 %fusion = f32[1,4,128,128]{3,0,2,1:T(1,128)S(1)} fusion(bf16[64,4,128,128]{3,2,1,0:T(8,128)(2,1)} %bitcast.149, s32[]{:T(128)S(6)} %axis_index.15), kind=kOutput, calls=%fused_computation | convolution fusion | flops 8388672 | bytes 8650756 | tf_op jit(solution)/shard_map/n,nhde->hde/dot_general | solution.py:61
  212.3 1.3 copy.25
  215.3 1.3 copy.24
  (106 shorter events, 16.5 us)
Async XLA Ops:
  7.2 2.4 %copy-start.23 = (bf16[1024,512]{1,0:T(8,128)(2,1)S(1)}, bf16[1024,512]{1,0:T(8,128)(2,1)}, u32[]{:S(2)}) copy-start(bf16[1024,512]{1,0:T(8,128)(2,1)} %param.7) | copy-start | bytes 3145732
  7.2 92.2 %all-gather.5.cloned.1.call-start = ((), (), s32[]{:S(2)}) async-start(), calls=%async_computation | async-start | bytes 8519680 | tf_op jit(solution)/shard_map/all_gather | solution.py:22
  9.6 4.0 %copy-start.6 = (bf16[1024,512]{1,0:T(8,128)(2,1)S(1)}, bf16[1024,512]{1,0:T(8,128)(2,1)}, u32[]{:S(2)}) copy-start(bf16[1024,512]{1,0:T(8,128)(2,1)} %param.6) | copy-start | bytes 3145732
  9.6 4.0 %copy-start.19 = (bf16[1024,512]{1,0:T(8,128)(2,1)S(1)}, bf16[1024,512]{1,0:T(8,128)(2,1)}, u32[]{:S(2)}) copy-start(bf16[1024,512]{1,0:T(8,128)(2,1)} %param.5) | copy-start | bytes 3145732
  12.1 190.5 %all-gather.7.cloned.1.call-start = ((), (), s32[]{:S(2)}) async-start(), calls=%async_computation.1 | async-start | bytes 8519680 | tf_op jit(solution)/shard_map/all_gather | solution.py:58
  14.4 2.3 %copy-start.9 = (bf16[1024,1024]{1,0:T(8,128)(2,1)}, bf16[1024,1024]{1,0:T(8,128)(2,1)S(1)}, u32[]{:S(2)}) copy-start(bf16[1024,1024]{1,0:T(8,128)(2,1)S(1)} %select_convert_fusion.5) | copy-start | bytes 6291460
  15.2 3.5 %copy-start.13 = (bf16[1024,1024]{1,0:T(8,128)(2,1)}, bf16[1024,1024]{1,0:T(8,128)(2,1)S(1)}, u32[]{:S(2)}) copy-start(bf16[1024,1024]{1,0:T(8,128)(2,1)S(1)} %select_convert_fusion.6) | copy-start | bytes 6291460
  15.9 4.4 %copy-start.15 = (bf16[1024,1024]{1,0:T(8,128)(2,1)}, bf16[1024,1024]{1,0:T(8,128)(2,1)S(1)}, u32[]{:S(2)}) copy-start(bf16[1024,1024]{1,0:T(8,128)(2,1)S(1)} %select_convert_fusion.7) | copy-start | bytes 6291460
  15.9 1.9 copy-start.24
  17.9 3.3 %copy-start.11 = (bf16[1024,1024]{1,0:T(8,128)(2,1)}, bf16[1024,1024]{1,0:T(8,128)(2,1)S(1)}, u32[]{:S(2)}) copy-start(bf16[1024,1024]{1,0:T(8,128)(2,1)S(1)} %select_convert_fusion.4) | copy-start | bytes 6291460
  99.3 8.1 %copy-start.20 = (bf16[1024,512]{1,0:T(8,128)(2,1)S(1)}, bf16[1024,512]{1,0:T(8,128)(2,1)}, u32[]{:S(2)}) copy-start(bf16[1024,512]{1,0:T(8,128)(2,1)} %param.5) | copy-start | bytes 3145732
  118.6 2.9 %copy-start.21 = (bf16[1024,512]{1,0:T(8,128)(2,1)S(1)}, bf16[1024,512]{1,0:T(8,128)(2,1)}, u32[]{:S(2)}) copy-start(bf16[1024,512]{1,0:T(8,128)(2,1)} %param.5) | copy-start | bytes 3145732
  121.5 1.2 copy-start.18
  124.1 1.8 copy-start.7
  125.9 1.2 copy-start.25
  127.9 1.9 copy-start
  129.8 1.9 copy-start.2
  131.7 1.3 copy-start.4
  136.6 3.0 %copy-start.14 = (bf16[1024,1024]{1,0:T(8,128)(2,1)S(1)}, bf16[1024,1024]{1,0:T(8,128)(2,1)}, u32[]{:S(2)}) copy-start(bf16[1024,1024]{1,0:T(8,128)(2,1)} %copy-done.13) | copy-start | bytes 6291460
  139.6 1.8 copy-start.10
  141.4 1.8 copy-start.12
  143.2 1.3 copy-start.22
  144.4 1.8 copy-start.1
  146.2 1.6 copy-start.3
  147.8 1.8 copy-start.5
  202.5 8.2 %copy-start.8 = (bf16[1024,512]{1,0:T(8,128)(2,1)S(1)}, bf16[1024,512]{1,0:T(8,128)(2,1)}, u32[]{:S(2)}) copy-start(bf16[1024,512]{1,0:T(8,128)(2,1)} %param.6) | copy-start | bytes 3145732
  202.6 8.2 %copy-start.33 = (f32[1024,128]{0,1:T(8,128)S(1)}, f32[1024,128]{0,1:T(8,128)}, u32[]{:S(2)}) copy-start(f32[1024,128]{0,1:T(8,128)} %fusion.34) | copy-start | bytes 1572868
  202.6 8.4 %copy-start.32 = (f32[1024,128]{0,1:T(8,128)S(1)}, f32[1024,128]{0,1:T(8,128)}, u32[]{:S(2)}) copy-start(f32[1024,128]{0,1:T(8,128)} %fusion.38) | copy-start | bytes 1572868
  210.7 1.3 copy-start.30
  212.2 1.4 copy-start.26
  212.2 1.5 copy-start.27
  213.7 1.3 copy-start.29
  (6 other events, 5.5 us)
Sparse Core Ops, SparseCore 0:
  12.2 87.1 all-gather.4
  122.8 79.6 all-gather.6
where the time goes:
time: 224 us; the launch traced here: 223 us
  waiting for transfers between devices  129 us (58%)
  matrix products  48.6 us (22%)
  local copies, waits for them, and re-layouts  18 us (8%)
  between operations  14.6 us (7%)
  blocking collectives  8.54 us (4%)
  other arithmetic  4.56 us (2%)
    all_gather x1, waiting for transfers between devices, shards(): piece = lax.all_gather(block_state[None], 'seq', axis=0, tiled=True)  77.3 us
    all_gather x1, waiting for transfers between devices, shards(): piece = lax.all_gather(query_term[None], 'seq', axis=0, tiled=True)  51.7 us
    dot_general x2, matrix products, shards(): jnp.einsum('n,nhde->hde', select, piece, preferred_element_type=jnp.float32)  16.2 us
    unnamed x77, local copies, waits for them, and re-layouts  14.9 us
    psum x1, blocking collectives, shards(): square_total = lax.psum(squares, 'head')  8.54 us
    dot_general x4, matrix products, shards(): jnp.dot(head_weights[head_number].T, grad_head, preferred_element_type=jn...  6.77 us
  transfers between devices with their start and end apart: 2, of which 2 were waited for; matrix products, arithmetic and copies ran while one was open for 15% of the time, Pallas kernels for 0%

commit v1 on v0

--- a/solution.py
+++ b/solution.py
@@ -6,6 +6,12 @@
 HEAD_DIM = 128
 WIDTH = 2048
 epsilon = 1e-06
+pair_pairs_all = lambda unit: jnp.concatenate(
+    lax.all_to_all(
+        jnp.stack([unit] * lax.axis_size("seq")), axis_name="seq", split_axis=0, concat_axis=0
+    ),
+    axis=0,
+)
 
 
 def shards(queries, key_vectors, value_vectors, cotangent, norm_gain):
@@ -19,7 +25,7 @@
         "thd,the->hde", shaped_k, shaped_v, preferred_element_type=jnp.float32
     ).astype(jnp.bfloat16)
     position = lax.axis_index("seq")
-    piece = lax.all_gather(block_state[None], "seq", axis=0, tiled=True)
+    piece = pair_pairs_all(block_state[None])
     owners = jnp.arange(piece.shape[0], dtype=jnp.int32)
     select = (owners < position).astype(jnp.bfloat16)
     prefix = jnp.einsum("n,nhde->hde", select, piece, preferred_element_type=jnp.float32)

time: 224 us -> 340 us (1.52)
  waiting for transfers between devices: 129 us -> 226 us
  starting transfers between devices: 0.08 us -> 13.4 us
  local copies, waits for them, and re-layouts: 18 us -> 24.1 us
    all_to_all x0 -> x1, waiting for transfers between devices: none -> 172 us  [lax.all_to_all(jnp.stack([unit] * lax.axis_size('seq')), axis_name='seq',...]
    all_gather x1 -> x0, waiting for transfers between devices: 77.3 us -> none  [shards(): piece = lax.all_gather(block_state[None], 'seq', axis=0, tiled=True)]
    all_to_all x0 -> x1, starting transfers between devices: none -> 13.2 us  [lax.all_to_all(jnp.stack([unit] * lax.axis_size('seq')), axis_name='seq',...]
    another operation x0 -> x1, local copies, waits for them, and re-layouts: none -> 5.37 us  [jnp.stack([unit] * lax.axis_size('seq'))]
    unnamed x77 -> x75, local copies, waits for them, and re-layouts: 14.9 us -> 16.3 us
  transfers between devices with their start and end apart: 2 -> 2, of which waited for: 2 -> 2; matrix products, arithmetic and copies ran while one was open for 15% -> 10% of each run, Pallas kernels for 0% -> 0%
where the time goes in v1:
time: 340 us; the launch traced here: 339 us
  waiting for transfers between devices  226 us (66%)
  matrix products  47.5 us (14%)
  local copies, waits for them, and re-layouts  24.1 us (7%)
  between operations  14.6 us (4%)
  starting transfers between devices  13.4 us (4%)
  blocking collectives  9.03 us (3%)
  other arithmetic  4.57 us (1%)
    all_to_all x1, waiting for transfers between devices, lax.all_to_all(jnp.stack([unit] * lax.axis_size('seq')), axis_name='seq',...  172 us
    all_gather x1, waiting for transfers between devices, shards(): piece = lax.all_gather(query_term[None], 'seq', axis=0, tiled=True)  53.8 us
    unnamed x75, local copies, waits for them, and re-layouts  16.3 us
    dot_general x2, matrix products, shards(): jnp.einsum('n,nhde->hde', select, piece, preferred_element_type=jnp.float32)  16.2 us
    all_to_all x1, starting transfers between devices, lax.all_to_all(jnp.stack([unit] * lax.axis_size('seq')), axis_name='seq',...  13.2 us
    psum x1, blocking collectives, shards(): square_total = lax.psum(squares, 'head')  9.03 us
  transfers between devices with their start and end apart: 2, of which 2 were waited for; matrix products, arithmetic and copies ran while one was open for 10% of the time, Pallas kernels for 0%

profile of v1, /device:TPU:1, one launch (start us, length us, event | category | flops | bytes accessed | tf_op | source)
XLA Modules:
  0.0 338.9 jit_solution(12007786141518109728)
XLA Ops:
  7.2 1.6 copy.32
  9.2 5.4 %stack.3 = bf16[64,1,4,128,128]{4,3,2,1,0:T(8,128)(2,1)} broadcast(bf16[4,128,128]{2,1,0:T(8,128)(2,1)S(1)} %convolution_convert_fusion.1), dimensions={2,3,4} | broadcast | bytes 8519680 | tf_op jit(solution)/shard_map/stack | solution.py:11
  14.6 13.2 %all-to-all-start = ((bf16[64,1,4,128,128]{4,3,2,1,0:T(8,128)(2,1)}), bf16[64,1,4,128,128]{4,3,2,1,0:T(8,128)(2,1)}, u32[]{:S(2)}, u32[]{:S(2)}) async-start(bf16[64,1,4,128,128]{4,3,2,1,0:T(8,128)(2,1)} %stack.3), calls=%async_computation | async-start | bytes 16777216 | tf_op jit(solution)/shard_map/all_to_all | solution.py:10
  28.0 1.6 copy.19
  32.7 1.1 copy-done.23
  34.7 1.6 fusion.63
  36.3 0.8 fusion.75
  37.2 0.8 fusion.87
  38.0 172.0 %all-to-all-done = bf16[64,1,4,128,128]{4,3,2,1,0:T(8,128)(2,1)} async-done(((bf16[64,1,4,128,128]{4,3,2,1,0:T(8,128)(2,1)}), bf16[64,1,4,128,128]{4,3,2,1,0:T(8,128)(2,1)}, u32[]{:S(2)}, u32[]{:S(2)}) %all-to-all-start) | async-done | bytes 8388640 | tf_op jit(solution)/shard_map/all_to_all | solution.py:10
  210.0 8.1 %fusion.2 = f32[1,4,128,128]{3,0,2,1:T(1,128)S(1)} fusion(bf16[64,4,128,128]{3,2,1,0:T(8,128)(2,1)} %bitcast.3, s32[]{:T(128)S(6)} %axis_index.15), kind=kOutput, calls=%fused_computation.2 | convolution fusion | flops 8388672 | bytes 8650756 | tf_op jit(solution)/shard_map/n,nhde->hde/dot_general | solution.py:31
  220.7 9.0 %all-reduce = (f32[1024]{0:T(1024)S(1)}, f32[1024]{0:T(1024)S(1)}) all-reduce(f32[1024]{0:T(1024)S(1)} %get-tuple-element.13, f32[1024]{0:T(1024)S(1)} %get-tuple-element.12), channel_id=1, replica_groups=mesh['seq'=64,'head'=4] {'head'}, use_global_device_ids=true, to_apply=%region_1.2 | all-reduce | flops 2048 | bytes 16384 | tf_op jit(solution)/shard_map/psum | solution.py:53
  229.8 2.9 multiply_convert_fusion
  233.9 1.7 select_convert_fusion.3
  235.7 1.9 fusion.90
  239.0 0.8 fusion.78
  240.9 0.8 fusion.66
  242.8 0.8 fusion.54
  244.4 1.0 pad_maximum_fusion.1
  245.4 2.3 copy.23
  247.7 2.3 copy.22
  250.0 3.0 fusion.46
  253.0 1.2 fusion.42
  254.7 1.3 fusion.38
  256.5 1.2 fusion.34
  257.8 1.3 fusion.93
  260.1 1.1 copy-done.3
  261.2 1.3 fusion.69
  262.9 1.3 fusion.57
  264.2 53.8 %all-gather.3.cloned.1.call-done = bf16[256,128,128]{2,1,0:T(8,128)(2,1)} async-done(((bf16[4,128,128]{2,1,0:T(8,128)(2,1)}), bf16[256,128,128]{2,1,0:T(8,128)(2,1)}) %all-gather.3.cloned.1.call-update) | async-done | bytes 8388624 | tf_op jit(solution)/shard_map/all_gather | solution.py:64
  318.0 8.1 %fusion = f32[1,4,128,128]{3,0,2,1:T(1,128)S(1)} fusion(bf16[64,4,128,128]{3,2,1,0:T(8,128)(2,1)} %bitcast.149, s32[]{:T(128)S(6)} %axis_index.15), kind=kOutput, calls=%fused_computation | convolution fusion | flops 8388672 | bytes 8650756 | tf_op jit(solution)/shard_map/n,nhde->hde/dot_general | solution.py:67
  327.8 1.3 copy.25
  330.8 1.3 copy.24
  (104 shorter events, 18.3 us)
Async XLA Ops:
  7.2 1.6 copy-start.22
  14.6 195.5 %all-to-all-start = ((bf16[64,1,4,128,128]{4,3,2,1,0:T(8,128)(2,1)}), bf16[64,1,4,128,128]{4,3,2,1,0:T(8,128)(2,1)}, u32[]{:S(2)}, u32[]{:S(2)}) async-start(bf16[64,1,4,128,128]{4,3,2,1,0:T(8,128)(2,1)} %stack.3), calls=%async_computation | async-start | bytes 16777216 | tf_op jit(solution)/shard_map/all_to_all | solution.py:10
  27.7 1.9 copy-start.6
  27.8 1.9 copy-start.18
  27.8 290.2 %all-gather.3.cloned.1.call-start = ((), (), s32[]{:S(2)}) async-start(), calls=%async_computation.1 | async-start | bytes 8519680 | tf_op jit(solution)/shard_map/all_gather | solution.py:64
  30.4 2.3 copy-start.9
  31.2 3.5 %copy-start.11 = (bf16[1024,1024]{1,0:T(8,128)(2,1)}, bf16[1024,1024]{1,0:T(8,128)(2,1)S(1)}, u32[]{:S(2)}) copy-start(bf16[1024,1024]{1,0:T(8,128)(2,1)S(1)} %select_convert_fusion.5) | copy-start | bytes 6291460
  31.9 4.4 %copy-start.13 = (bf16[1024,1024]{1,0:T(8,128)(2,1)}, bf16[1024,1024]{1,0:T(8,128)(2,1)S(1)}, u32[]{:S(2)}) copy-start(bf16[1024,1024]{1,0:T(8,128)(2,1)S(1)} %select_convert_fusion.6) | copy-start | bytes 6291460
  31.9 1.9 copy-start.23
  33.9 3.3 copy-start.15
  210.0 8.1 %copy-start.19 = (bf16[1024,512]{1,0:T(8,128)(2,1)S(1)}, bf16[1024,512]{1,0:T(8,128)(2,1)}, u32[]{:S(2)}) copy-start(bf16[1024,512]{1,0:T(8,128)(2,1)} %param.5) | copy-start | bytes 3145732
  218.1 1.0 copy-start.33
  229.8 2.9 copy-start.20
  235.6 2.1 copy-start.24
  237.8 1.2 copy-start.7
  239.0 1.9 copy-start
  240.9 1.9 copy-start.2
  242.8 1.4 copy-start.4
  250.0 3.0 copy-start.14
  253.0 1.8 copy-start.12
  254.7 1.8 copy-start.10
  256.5 1.2 copy-start.21
  257.8 1.8 copy-start.1
  259.6 1.6 copy-start.3
  261.1 1.8 copy-start.5
  318.0 8.2 %copy-start.8 = (bf16[1024,512]{1,0:T(8,128)(2,1)S(1)}, bf16[1024,512]{1,0:T(8,128)(2,1)}, u32[]{:S(2)}) copy-start(bf16[1024,512]{1,0:T(8,128)(2,1)} %param.6) | copy-start | bytes 3145732
  318.0 8.2 %copy-start.29 = (f32[1024,128]{0,1:T(8,128)S(1)}, f32[1024,128]{0,1:T(8,128)}, u32[]{:S(2)}) copy-start(f32[1024,128]{0,1:T(8,128)} %fusion.46) | copy-start | bytes 1572868
  318.0 8.4 %copy-start.30 = (f32[1024,128]{0,1:T(8,128)S(1)}, f32[1024,128]{0,1:T(8,128)}, u32[]{:S(2)}) copy-start(f32[1024,128]{0,1:T(8,128)} %fusion.42) | copy-start | bytes 1572868
  326.1 1.3 copy-start.32
  327.7 1.4 copy-start.25
  327.7 1.5 copy-start.26
  329.2 1.3 copy-start.28
  (5 other events, 4.5 us)
Sparse Core Ops, SparseCore 0:
  234.0 83.9 all-gather.2
